TPU v7x, 32 devices: a whole 2x2x4 slice. The times are simulated.
32 devices in a mesh: seg: 4 (over y, x), bin: 8 (over z, core).
Axes of the slice: x: 2, y: 2, z: 4, core: 2. Of those that a mesh axis runs over, the one named last changes fastest.
Arguments:
- coverage_lanes: bfloat16 [256, 128, 128], P(('seg', 'bin')), may hold values from 4 to 64
- target_blocks: int32 [256], P(('seg', 'bin')), may hold values from 0 to 7, as said below
- valid_bins: int32 [256], P(('seg', 'bin')), may hold values from 1 to 128
- panel_mean: float32 [32768], P(('seg', 'bin')), may hold values from 3.5 to 5
- components: float32 [256, 32768], P(None, ('seg', 'bin')), as said below
- kernels: float32 [3, 33, 32768], P(None, None, ('seg', 'bin')), may hold values from 0 to 0.08
- chrom_starts: int32 [24], replicated, may hold values from 0 to 32767, as said below
Outputs:
- coefficients: float32 [128, 256], replicated
- smoothed: float32 [128, 32768], P(None, ('seg', 'bin'))
- bridge: float32 [128, 32768], P(None, ('seg', 'bin'))
Inputs may be any that keep to these rules, and one draw needn't show every extreme that they name: target_blocks names one of the owner's 8 blocks; slot r of a device goes to the owner given by r // 1 within the device's stretch. `chrom_starts`: strictly rising chromosome starts, the first is 0 and the last is 32767. panel-of-normals components.
All inputs are finite; a program needn't handle non-finite values.
Results may differ from a plain program's by a relative error of at most 0.0003.
Values may be sent and summed in bfloat16 or wider, within the bound.
A program may use at most 192 MiB of HBM per device.

v0:
```python
import math
import jax
import jax.numpy as jnp
from jax import lax
from jax.sharding import PartitionSpec as P


def extended(block, sides, width):
    for axis, dim in sides:
        count = lax.axis_size(axis)
        forward = [(i, i + 1) for i in range(count - 1)]
        backward = [(target, source) for source, target in forward]
        low = lax.ppermute(
            lax.slice_in_dim(block, block.shape[dim] - width, None, axis=dim), axis, forward
        )
        high = lax.ppermute(lax.slice_in_dim(block, 0, width, axis=dim), axis, backward)
        block = jnp.concatenate([low, block, high], axis=dim)
    return block


def prefix(part, axis, combine, identity):
    place = lax.axis_index(axis)
    gathered = lax.all_gather(part, axis)
    state = jnp.zeros_like(part) + jnp.asarray(identity, part.dtype)

    def one(hop, state):
        return combine(state, lax.dynamic_index_in_dim(gathered, hop, 0, False))

    return lax.fori_loop(0, place, one, state)


def chrom_labels(chrom_starts, first_bin, count, total_bins):
    positions = first_bin + lax.iota(jnp.int32, count)
    covered = jnp.sum((chrom_starts[:, None] <= positions[None, :]).astype(jnp.int32), axis=0) - 1
    return jnp.where(positions >= total_bins, chrom_starts.shape[0], covered)


def smooth_once(padded, tap_weights, labels, out_width):
    half_taps = (tap_weights.shape[0] - 1) // 2
    centre = labels[half_taps : half_taps + out_width]
    result = jnp.zeros((padded.shape[0], out_width), jnp.float32)
    for tap_index in range(tap_weights.shape[0]):
        weight = tap_weights[tap_index] * (
            labels[tap_index : tap_index + out_width] == centre
        ).astype(jnp.float32)
        result = result + weight[None, :] * padded[:, tap_index : tap_index + out_width]
    return result


def add_terms(earlier, later):
    return earlier + later


def per_device(
    coverage_lanes, target_blocks, valid_bins, panel_mean, components, kernels, chrom_starts
):
    slot_count, samples, block_bins = coverage_lanes.shape
    bin_dev = panel_mean.shape[0]
    blocks_dev = bin_dev // block_bins
    total_bins = bin_dev * lax.axis_size(("seg", "bin"))
    first_bin = lax.axis_index(("seg", "bin")) * bin_dev
    keep_mask = (lax.iota(jnp.int32, block_bins)[None, :] < valid_bins[:, None]).astype(
        jnp.bfloat16
    )
    masked = coverage_lanes * keep_mask[:, None, :]
    arrived, arrived_targets = (
        lax.all_to_all(masked, "bin", split_axis=0, concat_axis=0, tiled=True),
        lax.all_to_all(
            target_blocks.astype(jnp.bfloat16), "bin", split_axis=0, concat_axis=0, tiled=True
        ),
    )
    block_names = lax.iota(jnp.int32, blocks_dev).astype(jnp.bfloat16)
    placing = (arrived_targets[None, :] == block_names[:, None]).astype(jnp.bfloat16)
    coverage = jnp.einsum("br,rsc->sbc", placing, arrived, preferred_element_type=jnp.float32)
    coverage = coverage.reshape(samples, bin_dev)
    log_ratio = jnp.log(coverage + 1.0) - panel_mean[None, :]
    partial_terms = lax.dot_general(
        log_ratio,
        components,
        (((1,), (1,)), ((), ())),
        precision=lax.Precision.HIGHEST,
        preferred_element_type=jnp.float32,
    )
    coefficients = lax.psum(partial_terms, ("seg", "bin"))
    signal = log_ratio - jnp.dot(
        coefficients,
        components,
        precision=lax.Precision.HIGHEST,
        preferred_element_type=jnp.float32,
    )
    layers = kernels.shape[0]
    half_taps = (kernels.shape[1] - 1) // 2
    labels = chrom_labels(chrom_starts, first_bin - half_taps, bin_dev + 2 * half_taps, total_bins)
    smoothed = signal
    for layer_index in range(layers):
        padded = extended(smoothed, ((("seg", "bin"), 1),), half_taps)
        smoothed = smooth_once(padded, kernels[layer_index], labels, bin_dev)
    totals = lax.psum(jnp.sum(smoothed, axis=1), ("seg", "bin"))
    centred = smoothed - (totals / total_bins)[:, None]
    blocks_view = centred.reshape(samples, blocks_dev, block_bins)
    upper_ones = (
        lax.iota(jnp.int32, block_bins)[:, None] <= lax.iota(jnp.int32, block_bins)[None, :]
    ).astype(jnp.float32)
    inside = jnp.einsum(
        "snc,cd->snd",
        blocks_view,
        upper_ones,
        precision=lax.Precision.HIGHEST,
        preferred_element_type=jnp.float32,
    )
    block_sums = inside[:, :, -1]
    running = jnp.cumsum(block_sums, axis=1)
    local_prefix = inside + (running - block_sums)[:, :, None]
    local_total = running[:, -1]
    zero_terms = jnp.zeros_like(local_total)
    before = prefix(local_total, ("seg", "bin"), add_terms, zero_terms)
    bridge = (local_prefix.reshape(samples, bin_dev) + before[:, None]) * (
        1.0 / math.sqrt(total_bins)
    )
    return (coefficients, smoothed, bridge)


def solution(mesh):
    in_specs = (
        P(("seg", "bin"), None, None),
        P(("seg", "bin")),
        P(("seg", "bin")),
        P(("seg", "bin")),
        P(None, ("seg", "bin")),
        P(None, None, ("seg", "bin")),
        P(),
    )
    out_specs = (P(), P(None, ("seg", "bin")), P(None, ("seg", "bin")))
    return jax.shard_map(
        per_device, mesh=mesh, in_specs=in_specs, out_specs=out_specs, check_vma=False
    )
```

profile of v0, /device:TPU:5, one launch (start us, length us, event | category | flops | bytes accessed | tf_op | source)
XLA Modules:
  0.0 307.1 jit_solution(12977762061642653183)
XLA Ops:
  7.2 0.7 convert_bitcast_fusion
  7.9 0.7 copy.21
  8.6 5.5 %all-to-all-start.1 = ((bf16[8,1,1]{2,1,0:T(2,128)(2,1)}), bf16[8,1,1]{2,1,0:T(2,128)(2,1)S(1)}, u32[]{:S(2)}, u32[]{:S(2)}) async-start(bf16[8,1,1]{2,1,0:T(2,128)(2,1)} %copy.21), calls=%async_computation.1 | async-start | bytes 8192 | tf_op jit(solution)/shard_map/all_to_all | solution.py:68
  14.2 0.8 fusion.306
  15.0 1.4 fusion.303
  16.4 1.4 fusion.305
  17.8 1.4 fusion.302
  19.1 1.4 fusion.301
  20.5 1.7 fusion.304
  22.2 0.6 copy-done.5
  22.9 0.6 copy-done.6
  23.6 0.1 convert_reduce_fusion
  23.7 0.7 broadcast_multiply_fusion
  24.5 0.1 broadcast_select_fusion.27
  24.6 0.1 broadcast_select_fusion.95
  24.6 0.1 broadcast_select_fusion.28
  24.8 0.1 broadcast_select_fusion.30
  24.8 0.1 broadcast_select_fusion.29
  25.1 5.1 %all-to-all-start = ((bf16[8,128,128]{2,1,0:T(8,128)(2,1)}), bf16[8,128,128]{2,1,0:T(8,128)(2,1)S(1)}, u32[]{:S(2)}, u32[]{:S(2)}) async-start(bf16[8,128,128]{2,1,0:T(8,128)(2,1)} %broadcast_multiply_fusion), calls=%async_computation | async-start | bytes 524288 | tf_op jit(solution)/shard_map/all_to_all | solution.py:67
  30.2 0.1 reduce
  30.4 8.5 %all-to-all-done = bf16[8,128,128]{2,1,0:T(8,128)(2,1)S(1)} async-done(((bf16[8,128,128]{2,1,0:T(8,128)(2,1)}), bf16[8,128,128]{2,1,0:T(8,128)(2,1)S(1)}, u32[]{:S(2)}, u32[]{:S(2)}) %all-to-all-start) | async-done | bytes 262176 | tf_op jit(solution)/shard_map/all_to_all | solution.py:67
  38.9 0.3 fusion
  39.2 0.4 copy-done.4
  39.6 1.8 fusion.286
  41.5 121.1 %all-reduce.2.cloned.1.call-done = f32[128,256]{1,0:T(8,128)} async-done(((f32[128,256]{1,0:T(8,128)}), f32[128,256]{1,0:T(8,128)}) %all-reduce.2.cloned.1.call-update) | async-done | bytes 131088 | tf_op jit(solution)/shard_map/psum | solution.py:84
  162.5 1.7 convolution_subtract_fusion
  164.2 0.1 fusion.300
  164.3 4.3 %collective-permute-start = (f32[128,16]{1,0:T(8,128)S(1)}, f32[128,16]{1,0:T(8,128)S(1)}, u32[]{:S(2)}, u32[]{:S(2)}) collective-permute-start(f32[128,16]{1,0:T(8,128)S(1)} %get-tuple-element.105), channel_id=1, source_target_pairs={{0,1},{1,2},{2,3},{3,4},{4,5},{5,6},{6,7},{7,8},{8,9},{9,10},{10,1... | collective-permute-start | bytes 24584 | tf_op jit(solution)/shard_map/ppermute | solution.py:13
  168.6 1.9 collective-permute-start.1
  170.6 3.9 %collective-permute-done.1 = f32[128,16]{1,0:T(8,128)S(1)} collective-permute-done((f32[128,16]{1,0:T(8,128)S(1)}, f32[128,16]{1,0:T(8,128)S(1)}, u32[]{:S(2)}, u32[]{:S(2)}) %collective-permute-start.1) | collective-permute-done | bytes 8224 | tf_op jit(solution)/shard_map/ppermute | solution.py:16
  174.4 6.0 %fusion.188 = f32[128,1024]{1,0:T(8,128)S(1)} fusion(f32[128,1024]{1,0:T(8,128)S(1)} %convolution_subtract_fusion, f32[128,16]{1,0:T(8,128)S(1)} %collective-permute-done.1, f32[128,16]{1,0:T(8,128)S(1)} %collective-permute-done, f32[1024]{0:T(1024)S(1)} %get-tuple-element.321, f32[1024]{0:T(1024)S(1)} %get-tuple-element.319, ...), kind=kLoop, calls=%fused_computation.371 | loop fusion | flops 12713984 | bytes 1200128 | tf_op jit(solution)/shard_map/add | solution.py:46
  180.4 0.1 fusion.299
  180.5 1.9 collective-permute-start.2
  182.4 4.2 %collective-permute-start.3 = (f32[128,16]{1,0:T(8,128)S(1)}, f32[128,16]{1,0:T(8,128)S(1)}, u32[]{:S(2)}, u32[]{:S(2)}) collective-permute-start(f32[128,16]{1,0:T(8,128)S(1)} %get-tuple-element.104), channel_id=1, source_target_pairs={{1,0},{2,1},{3,2},{4,3},{5,4},{6,5},{7,6},{8,7},{9,8},{10,9},{11,1... | collective-permute-start | bytes 24584 | tf_op jit(solution)/shard_map/ppermute | solution.py:16
  186.6 1.4 collective-permute-done.3
  188.0 6.0 %fusion.96 = f32[128,1024]{1,0:T(8,128)S(1)} fusion(f32[128,1024]{1,0:T(8,128)S(1)} %fusion.188, f32[128,16]{1,0:T(8,128)S(1)} %collective-permute-done.3, f32[128,16]{1,0:T(8,128)S(1)} %collective-permute-done.2, f32[1024]{0:T(1024)S(1)} %get-tuple-element.320, f32[1024]{0:T(1024)S(1)} %get-tuple-element.318, f32[1024]{0:T(1024)S(1)} %get-tuple-element.325, ...), kind=kLoop, calls=%fused_computation.279 | loop fusion | flops 12713984 | bytes 1200128 | tf_op jit(solution)/shard_map/add | solution.py:46
  194.0 0.1 fusion.298
  194.1 1.9 collective-permute-start.4
  196.0 8.0 %collective-permute-start.5 = (f32[128,16]{1,0:T(8,128)S(1)}, f32[128,16]{1,0:T(8,128)S(1)}, u32[]{:S(2)}, u32[]{:S(2)}) collective-permute-start(f32[128,16]{1,0:T(8,128)S(1)} %get-tuple-element.102), channel_id=1, source_target_pairs={{1,0},{2,1},{3,2},{4,3},{5,4},{6,5},{7,6},{8,7},{9,8},{10,9},{11,1... | collective-permute-start | bytes 24584 | tf_op jit(solution)/shard_map/ppermute | solution.py:16
  204.0 0.7 collective-permute-done.5
  204.7 7.3 %fusion.296 = (f32[128]{0:T(128)S(1)}, f32[128,1024]{1,0:T(8,128)S(1)}) fusion(f32[128,16]{1,0:T(8,128)S(1)} %collective-permute-done.5, f32[128,1024]{1,0:T(8,128)S(1)} %fusion.96, f32[1024]{0:T(1024)S(1)} %get-tuple-element.256, f32[1024]{0:T(1024)S(1)} %get-tuple-element.206, f32[1024]{0:T(1024)S(1)} %get-tuple-element.208, ...), kind=kLoop, calls=%fused_computation.626 | loop fusion | flops 12844928 | bytes 1200640 | tf_op jit(solution)/shard_map/reduce_sum | solution.py:98
  212.0 43.9 %psum.15 = f32[128]{0:T(128)S(1)} all-reduce(f32[128]{0:T(128)S(1)} %get-tuple-element.35), channel_id=1, replica_groups=mesh['seg'=4,'bin'=8] {'seg','bin'}, use_global_device_ids=true, to_apply=%region_3.4 | all-reduce | flops 128 | bytes 1024 | tf_op jit(solution)/shard_map/psum | solution.py:98
  255.9 0.5 fusion.277
  256.5 0.2 copy.24
  256.7 41.3 %all-gather = f32[4096,1]{0,1:T(1,128)S(1)} all-gather(f32[128,1]{0,1:T(1,128)S(1)} %slice.1309), channel_id=2, replica_groups=mesh['seg'=4,'bin'=8] {'seg','bin'}, dimensions={0}, use_global_device_ids=true | all-gather | bytes 16896 | tf_op jit(solution)/shard_map/all_gather | solution.py:23
  298.1 0.6 while.10
  298.7 0.9 add_multiply_fusion
  299.6 0.7 copy.44
  (62 shorter events, 0.7 us)
Async XLA Ops:
  7.2 32.0 %copy-start = (f32[256,1024]{1,0:T(8,128)S(1)}, f32[256,1024]{1,0:T(8,128)}, u32[]{:S(2)}) copy-start(f32[256,1024]{1,0:T(8,128)} %param.13) | copy-start | bytes 3145732
  8.6 16.4 %all-to-all-start.1 = ((bf16[8,1,1]{2,1,0:T(2,128)(2,1)}), bf16[8,1,1]{2,1,0:T(2,128)(2,1)S(1)}, u32[]{:S(2)}, u32[]{:S(2)}) async-start(bf16[8,1,1]{2,1,0:T(2,128)(2,1)} %copy.21), calls=%async_computation.1 | async-start | bytes 8192 | tf_op jit(solution)/shard_map/all_to_all | solution.py:68
  17.8 5.9 %copy-start.3 = (bf16[8,128,128]{2,1,0:T(8,128)(2,1)S(1)}, bf16[8,128,128]{2,1,0:T(8,128)(2,1)}, u32[]{:S(2)}) copy-start(bf16[8,128,128]{2,1,0:T(8,128)(2,1)} %param.9) | copy-start | bytes 786436
  22.2 0.7 copy-start.5
  22.9 0.7 copy-start.6
  25.1 13.8 %all-to-all-start = ((bf16[8,128,128]{2,1,0:T(8,128)(2,1)}), bf16[8,128,128]{2,1,0:T(8,128)(2,1)S(1)}, u32[]{:S(2)}, u32[]{:S(2)}) async-start(bf16[8,128,128]{2,1,0:T(8,128)(2,1)} %broadcast_multiply_fusion), calls=%async_computation | async-start | bytes 524288 | tf_op jit(solution)/shard_map/all_to_all | solution.py:67
  30.2 132.4 %all-reduce.2.cloned.1.call-start = ((), (), s32[]{:S(2)}) async-start(), calls=%async_computation.2 | async-start | bytes 262144 | tf_op jit(solution)/shard_map/psum | solution.py:84
  38.9 0.7 copy-start.4
  164.3 6.3 %collective-permute-start = (f32[128,16]{1,0:T(8,128)S(1)}, f32[128,16]{1,0:T(8,128)S(1)}, u32[]{:S(2)}, u32[]{:S(2)}) collective-permute-start(f32[128,16]{1,0:T(8,128)S(1)} %get-tuple-element.105), channel_id=1, source_target_pairs={{0,1},{1,2},{2,3},{3,4},{4,5},{5,6},{6,7},{7,8},{8,9},{9,10},{10,1... | collective-permute-start | bytes 24584 | tf_op jit(solution)/shard_map/ppermute | solution.py:13
  168.6 5.8 %collective-permute-start.1 = (f32[128,16]{1,0:T(8,128)S(1)}, f32[128,16]{1,0:T(8,128)S(1)}, u32[]{:S(2)}, u32[]{:S(2)}) collective-permute-start(f32[128,16]{1,0:T(8,128)S(1)} %get-tuple-element.106), channel_id=1, source_target_pairs={{1,0},{2,1},{3,2},{4,3},{5,4},{6,5},{7,6},{8,7},{9,8},{10,9},{11,1... | collective-permute-start | bytes 24584 | tf_op jit(solution)/shard_map/ppermute | solution.py:16
  180.5 6.1 %collective-permute-start.2 = (f32[128,16]{1,0:T(8,128)S(1)}, f32[128,16]{1,0:T(8,128)S(1)}, u32[]{:S(2)}, u32[]{:S(2)}) collective-permute-start(f32[128,16]{1,0:T(8,128)S(1)} %get-tuple-element.103), channel_id=1, source_target_pairs={{0,1},{1,2},{2,3},{3,4},{4,5},{5,6},{6,7},{7,8},{8,9},{9,10},{10,1... | collective-permute-start | bytes 24584 | tf_op jit(solution)/shard_map/ppermute | solution.py:13
  182.4 5.6 %collective-permute-start.3 = (f32[128,16]{1,0:T(8,128)S(1)}, f32[128,16]{1,0:T(8,128)S(1)}, u32[]{:S(2)}, u32[]{:S(2)}) collective-permute-start(f32[128,16]{1,0:T(8,128)S(1)} %get-tuple-element.104), channel_id=1, source_target_pairs={{1,0},{2,1},{3,2},{4,3},{5,4},{6,5},{7,6},{8,7},{9,8},{10,9},{11,1... | collective-permute-start | bytes 24584 | tf_op jit(solution)/shard_map/ppermute | solution.py:16
  194.1 9.9 %collective-permute-start.4 = (f32[128,16]{1,0:T(8,128)S(1)}, f32[128,16]{1,0:T(8,128)S(1)}, u32[]{:S(2)}, u32[]{:S(2)}) collective-permute-start(f32[128,16]{1,0:T(8,128)S(1)} %get-tuple-element.101), channel_id=1, source_target_pairs={{0,1},{1,2},{2,3},{3,4},{4,5},{5,6},{6,7},{7,8},{8,9},{9,10},{10,1... | collective-permute-start | bytes 24584 | tf_op jit(solution)/shard_map/ppermute | solution.py:13
  196.0 8.7 %collective-permute-start.5 = (f32[128,16]{1,0:T(8,128)S(1)}, f32[128,16]{1,0:T(8,128)S(1)}, u32[]{:S(2)}, u32[]{:S(2)}) collective-permute-start(f32[128,16]{1,0:T(8,128)S(1)} %get-tuple-element.102), channel_id=1, source_target_pairs={{1,0},{2,1},{3,2},{4,3},{5,4},{6,5},{7,6},{8,7},{9,8},{10,9},{11,1... | collective-permute-start | bytes 24584 | tf_op jit(solution)/shard_map/ppermute | solution.py:16
  212.0 44.4 %copy-start.1 = (f32[128,1024]{1,0:T(8,128)}, f32[128,1024]{1,0:T(8,128)S(1)}, u32[]{:S(2)}) copy-start(f32[128,1024]{1,0:T(8,128)S(1)} %get-tuple-element.402) | copy-start | bytes 1572868
  298.7 0.9 copy-start.2
Sparse Core Ops, SparseCore 0:
  41.6 120.9 all-reduce.1
where the time goes:
time: 308 us; the launch traced here: 307 us
  waiting for transfers between devices  136 us (44%)
  blocking collectives  85.2 us (28%)
  starting transfers between devices  32.9 us (11%)
  other arithmetic  22.9 us (7%)
  between operations  14.4 us (5%)
  local copies, waits for them, and re-layouts  11.5 us (4%)
  matrix products  4.3 us (1%)
    psum x1, waiting for transfers between devices, per_device(): coefficients = lax.psum(partial_terms, ('seg', 'bin'))  121 us
    psum x1, blocking collectives, per_device(): totals = lax.psum(jnp.sum(smoothed, axis=1), ('seg', 'bin'))  43.9 us
    all_gather x1, blocking collectives, prefix(): gathered = lax.all_gather(part, axis)  41.3 us
    ppermute x3, starting transfers between devices, extended(): lax.ppermute(lax.slice_in_dim(block, 0, width, axis=dim), axis, backward)  14.1 us
    add x2, other arithmetic, smooth_once(): result + weight[None, :] * padded[:, tap_index:tap_index + out_width]  12 us
    all_to_all x1, waiting for transfers between devices, per_device(): lax.all_to_all(masked, 'bin', split_axis=0, concat_axis=0, tiled=True)  8.52 us
    ppermute x3, starting transfers between devices, extended(): lax.ppermute(lax.slice_in_dim(block, block.shape[dim] - width, None, axis...  8.15 us
    slice x6, local copies, waits for them, and re-layouts, smooth_once(): tap_weights[tap_index]  7.96 us
  transfers between devices with their start and end apart: 9, of which 5 were waited for; matrix products, arithmetic and copies ran while one was open for 3% of the time, Pallas kernels for 0%

commit v1 on v0

--- a/solution.py
+++ b/solution.py
@@ -3,6 +3,7 @@
 import jax.numpy as jnp
 from jax import lax
 from jax.sharding import PartitionSpec as P
+from jax.lax import all_gather
 
 
 def extended(block, sides, width):
@@ -95,7 +96,7 @@
     for layer_index in range(layers):
         padded = extended(smoothed, ((("seg", "bin"), 1),), half_taps)
         smoothed = smooth_once(padded, kernels[layer_index], labels, bin_dev)
-    totals = lax.psum(jnp.sum(smoothed, axis=1), ("seg", "bin"))
+    totals = jnp.sum(all_gather(jnp.sum(smoothed, axis=1), axis_name=("seg", "bin")), axis=0)
     centred = smoothed - (totals / total_bins)[:, None]
     blocks_view = centred.reshape(samples, blocks_dev, block_bins)
     upper_ones = (

time: 308 us -> 304 us (0.987)
  blocking collectives: 85.2 us -> 80.6 us
    psum x1 -> x0, blocking collectives: 43.9 us -> none  [per_device(): totals = lax.psum(jnp.sum(smoothed, axis=1), ('seg', 'bin'))]
    all_gather x0 -> x1, blocking collectives: none -> 42.7 us  [per_device(): all_gather(jnp.sum(smoothed, axis=1), axis_name=('seg', 'bin'))]
    all_gather x1, blocking collectives: 41.3 us -> 37.9 us  [prefix(): gathered = lax.all_gather(part, axis)]
    reduce_sum x1 -> x2, other arithmetic: 7.3 us -> 7.35 us  [the longest x1 7.3 us: per_device(): jnp.sum(smoothed, axis=1)]
where the time goes in v1:
time: 304 us; the launch traced here: 303 us
  waiting for transfers between devices  136 us (45%)
  blocking collectives  80.6 us (27%)
  starting transfers between devices  32.9 us (11%)
  other arithmetic  23 us (8%)
  between operations  14.4 us (5%)
  local copies, waits for them, and re-layouts  11.5 us (4%)
  matrix products  4.3 us (1%)
    psum x1, waiting for transfers between devices, per_device(): coefficients = lax.psum(partial_terms, ('seg', 'bin'))  121 us
    all_gather x1, blocking collectives, per_device(): all_gather(jnp.sum(smoothed, axis=1), axis_name=('seg', 'bin'))  42.7 us
    all_gather x1, blocking collectives, prefix(): gathered = lax.all_gather(part, axis)  37.9 us
    ppermute x3, starting transfers between devices, extended(): lax.ppermute(lax.slice_in_dim(block, 0, width, axis=dim), axis, backward)  14.1 us
    add x2, other arithmetic, smooth_once(): result + weight[None, :] * padded[:, tap_index:tap_index + out_width]  12 us
    all_to_all x1, waiting for transfers between devices, per_device(): lax.all_to_all(masked, 'bin', split_axis=0, concat_axis=0, tiled=True)  8.52 us
    ppermute x3, starting transfers between devices, extended(): lax.ppermute(lax.slice_in_dim(block, block.shape[dim] - width, None, axis...  8.15 us
    slice x6, local copies, waits for them, and re-layouts, smooth_once(): tap_weights[tap_index]  7.96 us
  transfers between devices with their start and end apart: 9, of which 5 were waited for; matrix products, arithmetic and copies ran while one was open for 3% of the time, Pallas kernels for 0%

profile of v1, /device:TPU:5, one launch (start us, length us, event | category | flops | bytes accessed | tf_op | source)
XLA Modules:
  0.0 302.5 jit_solution(8277347619195395829)
XLA Ops:
  7.2 0.7 convert_bitcast_fusion
  7.9 0.7 copy.21
  8.6 5.5 %all-to-all-start.1 = ((bf16[8,1,1]{2,1,0:T(2,128)(2,1)}), bf16[8,1,1]{2,1,0:T(2,128)(2,1)S(1)}, u32[]{:S(2)}, u32[]{:S(2)}) async-start(bf16[8,1,1]{2,1,0:T(2,128)(2,1)} %copy.21), calls=%async_computation.1 | async-start | bytes 8192 | tf_op jit(solution)/shard_map/all_to_all | solution.py:69
  14.2 0.8 fusion.306
  15.0 1.4 fusion.303
  16.4 1.4 fusion.305
  17.8 1.4 fusion.302
  19.1 1.4 fusion.301
  20.5 1.7 fusion.304
  22.2 0.6 copy-done.5
  22.9 0.6 copy-done.6
  23.6 0.1 convert_reduce_fusion
  23.7 0.7 broadcast_multiply_fusion
  24.5 0.1 broadcast_select_fusion.27
  24.6 0.1 broadcast_select_fusion.95
  24.6 0.1 broadcast_select_fusion.28
  24.8 0.1 broadcast_select_fusion.30
  24.8 0.1 broadcast_select_fusion.29
  25.1 5.1 %all-to-all-start = ((bf16[8,128,128]{2,1,0:T(8,128)(2,1)}), bf16[8,128,128]{2,1,0:T(8,128)(2,1)S(1)}, u32[]{:S(2)}, u32[]{:S(2)}) async-start(bf16[8,128,128]{2,1,0:T(8,128)(2,1)} %broadcast_multiply_fusion), calls=%async_computation | async-start | bytes 524288 | tf_op jit(solution)/shard_map/all_to_all | solution.py:68
  30.2 0.1 reduce.1
  30.4 8.5 %all-to-all-done = bf16[8,128,128]{2,1,0:T(8,128)(2,1)S(1)} async-done(((bf16[8,128,128]{2,1,0:T(8,128)(2,1)}), bf16[8,128,128]{2,1,0:T(8,128)(2,1)S(1)}, u32[]{:S(2)}, u32[]{:S(2)}) %all-to-all-start) | async-done | bytes 262176 | tf_op jit(solution)/shard_map/all_to_all | solution.py:68
  38.9 0.3 fusion
  39.2 0.4 copy-done.4
  39.6 1.8 fusion.286
  41.5 121.1 %all-reduce.2.cloned.1.call-done = f32[128,256]{1,0:T(8,128)} async-done(((f32[128,256]{1,0:T(8,128)}), f32[128,256]{1,0:T(8,128)}) %all-reduce.2.cloned.1.call-update) | async-done | bytes 131088 | tf_op jit(solution)/shard_map/psum | solution.py:85
  162.5 1.7 convolution_subtract_fusion
  164.2 0.1 fusion.300
  164.3 4.3 %collective-permute-start = (f32[128,16]{1,0:T(8,128)S(1)}, f32[128,16]{1,0:T(8,128)S(1)}, u32[]{:S(2)}, u32[]{:S(2)}) collective-permute-start(f32[128,16]{1,0:T(8,128)S(1)} %get-tuple-element.105), channel_id=1, source_target_pairs={{0,1},{1,2},{2,3},{3,4},{4,5},{5,6},{6,7},{7,8},{8,9},{9,10},{10,1... | collective-permute-start | bytes 24584 | tf_op jit(solution)/shard_map/ppermute | solution.py:14
  168.6 1.9 collective-permute-start.1
  170.6 3.9 %collective-permute-done.1 = f32[128,16]{1,0:T(8,128)S(1)} collective-permute-done((f32[128,16]{1,0:T(8,128)S(1)}, f32[128,16]{1,0:T(8,128)S(1)}, u32[]{:S(2)}, u32[]{:S(2)}) %collective-permute-start.1) | collective-permute-done | bytes 8224 | tf_op jit(solution)/shard_map/ppermute | solution.py:17
  174.4 6.0 %fusion.188 = f32[128,1024]{1,0:T(8,128)S(1)} fusion(f32[128,1024]{1,0:T(8,128)S(1)} %convolution_subtract_fusion, f32[128,16]{1,0:T(8,128)S(1)} %collective-permute-done.1, f32[128,16]{1,0:T(8,128)S(1)} %collective-permute-done, f32[1024]{0:T(1024)S(1)} %get-tuple-element.321, f32[1024]{0:T(1024)S(1)} %get-tuple-element.319, ...), kind=kLoop, calls=%fused_computation.371 | loop fusion | flops 12713984 | bytes 1200128 | tf_op jit(solution)/shard_map/add | solution.py:47
  180.4 0.1 fusion.299
  180.5 1.9 collective-permute-start.2
  182.4 4.2 %collective-permute-start.3 = (f32[128,16]{1,0:T(8,128)S(1)}, f32[128,16]{1,0:T(8,128)S(1)}, u32[]{:S(2)}, u32[]{:S(2)}) collective-permute-start(f32[128,16]{1,0:T(8,128)S(1)} %get-tuple-element.104), channel_id=1, source_target_pairs={{1,0},{2,1},{3,2},{4,3},{5,4},{6,5},{7,6},{8,7},{9,8},{10,9},{11,1... | collective-permute-start | bytes 24584 | tf_op jit(solution)/shard_map/ppermute | solution.py:17
  186.6 1.4 collective-permute-done.3
  188.0 6.0 %fusion.96 = f32[128,1024]{1,0:T(8,128)S(1)} fusion(f32[128,1024]{1,0:T(8,128)S(1)} %fusion.188, f32[128,16]{1,0:T(8,128)S(1)} %collective-permute-done.3, f32[128,16]{1,0:T(8,128)S(1)} %collective-permute-done.2, f32[1024]{0:T(1024)S(1)} %get-tuple-element.320, f32[1024]{0:T(1024)S(1)} %get-tuple-element.318, f32[1024]{0:T(1024)S(1)} %get-tuple-element.325, ...), kind=kLoop, calls=%fused_computation.279 | loop fusion | flops 12713984 | bytes 1200128 | tf_op jit(solution)/shard_map/add | solution.py:47
  194.0 0.1 fusion.298
  194.1 1.9 collective-permute-start.4
  196.0 8.0 %collective-permute-start.5 = (f32[128,16]{1,0:T(8,128)S(1)}, f32[128,16]{1,0:T(8,128)S(1)}, u32[]{:S(2)}, u32[]{:S(2)}) collective-permute-start(f32[128,16]{1,0:T(8,128)S(1)} %get-tuple-element.102), channel_id=1, source_target_pairs={{1,0},{2,1},{3,2},{4,3},{5,4},{6,5},{7,6},{8,7},{9,8},{10,9},{11,1... | collective-permute-start | bytes 24584 | tf_op jit(solution)/shard_map/ppermute | solution.py:17
  204.0 0.7 collective-permute-done.5
  204.7 7.3 %fusion.296 = (f32[128]{0:T(128)S(1)}, f32[128,1024]{1,0:T(8,128)S(1)}) fusion(f32[128,16]{1,0:T(8,128)S(1)} %collective-permute-done.5, f32[128,1024]{1,0:T(8,128)S(1)} %fusion.96, f32[1024]{0:T(1024)S(1)} %get-tuple-element.256, f32[1024]{0:T(1024)S(1)} %get-tuple-element.206, f32[1024]{0:T(1024)S(1)} %get-tuple-element.208, ...), kind=kLoop, calls=%fused_computation.626 | loop fusion | flops 12844928 | bytes 1200640 | tf_op jit(solution)/shard_map/reduce_sum | solution.py:99
  212.0 42.7 %all-gather.2 = f32[32,1,128]{2,1,0:T(1,128)S(1)} all-gather(f32[1,1,128]{2,1,0:T(1,128)S(1)} %bitcast.240), channel_id=2, replica_groups=mesh['seg'=4,'bin'=8] {'seg','bin'}, dimensions={0}, use_global_device_ids=true | all-gather | bytes 16896 | tf_op jit(solution)/shard_map/all_gather | solution.py:99
  254.8 0.5 fusion.277
  255.4 0.2 copy.24
  255.6 37.9 %all-gather.1 = f32[4096,1]{0,1:T(1,128)S(1)} all-gather(f32[128,1]{0,1:T(1,128)S(1)} %slice.1309), channel_id=3, replica_groups=mesh['seg'=4,'bin'=8] {'seg','bin'}, dimensions={0}, use_global_device_ids=true | all-gather | bytes 16896 | tf_op jit(solution)/shard_map/all_gather | solution.py:24
  293.5 0.6 while.10
  294.1 0.9 add_multiply_fusion
  295.0 0.7 copy.44
  (63 shorter events, 0.8 us)
Async XLA Ops:
  7.2 32.0 %copy-start = (f32[256,1024]{1,0:T(8,128)S(1)}, f32[256,1024]{1,0:T(8,128)}, u32[]{:S(2)}) copy-start(f32[256,1024]{1,0:T(8,128)} %param.13) | copy-start | bytes 3145732
  8.6 16.4 %all-to-all-start.1 = ((bf16[8,1,1]{2,1,0:T(2,128)(2,1)}), bf16[8,1,1]{2,1,0:T(2,128)(2,1)S(1)}, u32[]{:S(2)}, u32[]{:S(2)}) async-start(bf16[8,1,1]{2,1,0:T(2,128)(2,1)} %copy.21), calls=%async_computation.1 | async-start | bytes 8192 | tf_op jit(solution)/shard_map/all_to_all | solution.py:69
  17.8 5.9 %copy-start.3 = (bf16[8,128,128]{2,1,0:T(8,128)(2,1)S(1)}, bf16[8,128,128]{2,1,0:T(8,128)(2,1)}, u32[]{:S(2)}) copy-start(bf16[8,128,128]{2,1,0:T(8,128)(2,1)} %param.9) | copy-start | bytes 786436
  22.2 0.7 copy-start.5
  22.9 0.7 copy-start.6
  25.1 13.8 %all-to-all-start = ((bf16[8,128,128]{2,1,0:T(8,128)(2,1)}), bf16[8,128,128]{2,1,0:T(8,128)(2,1)S(1)}, u32[]{:S(2)}, u32[]{:S(2)}) async-start(bf16[8,128,128]{2,1,0:T(8,128)(2,1)} %broadcast_multiply_fusion), calls=%async_computation | async-start | bytes 524288 | tf_op jit(solution)/shard_map/all_to_all | solution.py:68
  30.2 132.4 %all-reduce.2.cloned.1.call-start = ((), (), s32[]{:S(2)}) async-start(), calls=%async_computation.2 | async-start | bytes 262144 | tf_op jit(solution)/shard_map/psum | solution.py:85
  38.9 0.7 copy-start.4
  164.3 6.3 %collective-permute-start = (f32[128,16]{1,0:T(8,128)S(1)}, f32[128,16]{1,0:T(8,128)S(1)}, u32[]{:S(2)}, u32[]{:S(2)}) collective-permute-start(f32[128,16]{1,0:T(8,128)S(1)} %get-tuple-element.105), channel_id=1, source_target_pairs={{0,1},{1,2},{2,3},{3,4},{4,5},{5,6},{6,7},{7,8},{8,9},{9,10},{10,1... | collective-permute-start | bytes 24584 | tf_op jit(solution)/shard_map/ppermute | solution.py:14
  168.6 5.8 %collective-permute-start.1 = (f32[128,16]{1,0:T(8,128)S(1)}, f32[128,16]{1,0:T(8,128)S(1)}, u32[]{:S(2)}, u32[]{:S(2)}) collective-permute-start(f32[128,16]{1,0:T(8,128)S(1)} %get-tuple-element.106), channel_id=1, source_target_pairs={{1,0},{2,1},{3,2},{4,3},{5,4},{6,5},{7,6},{8,7},{9,8},{10,9},{11,1... | collective-permute-start | bytes 24584 | tf_op jit(solution)/shard_map/ppermute | solution.py:17
  180.5 6.1 %collective-permute-start.2 = (f32[128,16]{1,0:T(8,128)S(1)}, f32[128,16]{1,0:T(8,128)S(1)}, u32[]{:S(2)}, u32[]{:S(2)}) collective-permute-start(f32[128,16]{1,0:T(8,128)S(1)} %get-tuple-element.103), channel_id=1, source_target_pairs={{0,1},{1,2},{2,3},{3,4},{4,5},{5,6},{6,7},{7,8},{8,9},{9,10},{10,1... | collective-permute-start | bytes 24584 | tf_op jit(solution)/shard_map/ppermute | solution.py:14
  182.4 5.6 %collective-permute-start.3 = (f32[128,16]{1,0:T(8,128)S(1)}, f32[128,16]{1,0:T(8,128)S(1)}, u32[]{:S(2)}, u32[]{:S(2)}) collective-permute-start(f32[128,16]{1,0:T(8,128)S(1)} %get-tuple-element.104), channel_id=1, source_target_pairs={{1,0},{2,1},{3,2},{4,3},{5,4},{6,5},{7,6},{8,7},{9,8},{10,9},{11,1... | collective-permute-start | bytes 24584 | tf_op jit(solution)/shard_map/ppermute | solution.py:17
  194.1 9.9 %collective-permute-start.4 = (f32[128,16]{1,0:T(8,128)S(1)}, f32[128,16]{1,0:T(8,128)S(1)}, u32[]{:S(2)}, u32[]{:S(2)}) collective-permute-start(f32[128,16]{1,0:T(8,128)S(1)} %get-tuple-element.101), channel_id=1, source_target_pairs={{0,1},{1,2},{2,3},{3,4},{4,5},{5,6},{6,7},{7,8},{8,9},{9,10},{10,1... | collective-permute-start | bytes 24584 | tf_op jit(solution)/shard_map/ppermute | solution.py:14
  196.0 8.7 %collective-permute-start.5 = (f32[128,16]{1,0:T(8,128)S(1)}, f32[128,16]{1,0:T(8,128)S(1)}, u32[]{:S(2)}, u32[]{:S(2)}) collective-permute-start(f32[128,16]{1,0:T(8,128)S(1)} %get-tuple-element.102), channel_id=1, source_target_pairs={{1,0},{2,1},{3,2},{4,3},{5,4},{6,5},{7,6},{8,7},{9,8},{10,9},{11,1... | collective-permute-start | bytes 24584 | tf_op jit(solution)/shard_map/ppermute | solution.py:17
  212.0 43.3 %copy-start.1 = (f32[128,1024]{1,0:T(8,128)}, f32[128,1024]{1,0:T(8,128)S(1)}, u32[]{:S(2)}) copy-start(f32[128,1024]{1,0:T(8,128)S(1)} %get-tuple-element.402) | copy-start | bytes 1572868
  294.1 0.9 copy-start.2
Sparse Core Ops, SparseCore 0:
  41.6 120.9 all-reduce.1
